TPU v7x, 32 devices: a whole 2x2x4 slice. The times are simulated.
32 devices in a mesh: layer: 4 (over y, x), lat: 8 (over z, core).
Axes of the slice: x: 2, y: 2, z: 4, core: 2. Of those that a mesh axis runs over, the one named last changes fastest.
Arguments:
- activations: bfloat16 [8, 512, 2048], P(None, None, 'layer'), may hold values from -6 to 6
- targets: bfloat16 [8, 512, 2048], P(None, None, 'layer'), may hold values from -6 to 6
- encoder: bfloat16 [8, 2048, 8192], P(None, 'layer', 'lat'), may hold values from -0.125 to 0.125
- bias: float32 [8, 8192], P(None, 'lat'), may hold values from -3 to 3
- decoder: bfloat16 [36, 8192, 2048], P(None, 'lat', 'layer'), may hold values from -0.75 to 0.75
- active: int32 [8, 512, 64], replicated, may hold values from 0 to 8191, all different within a row
Outputs:
- grad_encoder: bfloat16 [8, 2048, 8192], P(None, 'layer', 'lat')
- grad_bias: float32 [8, 8192], P(None, 'lat')
- grad_decoder: bfloat16 [36, 8192, 2048], P(None, 'lat', 'layer')
Inputs may be any that keep to these rules, and one draw needn't show every extreme that they name: `active`: each row names 64 different latents.
All inputs are finite; a program needn't handle non-finite values.
Results may differ from a plain program's by a relative error of at most 0.0064.
Values may be sent and summed in bfloat16 or wider, within the bound.
A program may use at most 256 MiB of HBM per device.

v0:
```python
import jax
import jax.numpy as jnp
from jax import lax
from jax.sharding import PartitionSpec as P

LAYERS = 8


def pair_index(source, target):
    return source * LAYERS - source * (source - 1) // 2 + (target - source)


def on_device(activations, targets, encoder, bias, decoder, active):
    tokens = activations.shape[1]
    lat_width = encoder.shape[2]
    first = lax.axis_index("lat") * lat_width
    columns = first + jnp.arange(lat_width, dtype=jnp.int32)
    masks = jnp.stack(
        [
            jnp.any(active[source][:, :, None] == columns[None, None, :], axis=1)
            for source in range(LAYERS)
        ]
    ).astype(jnp.float32)
    partial_value = jnp.einsum(
        "ltd,ldf->ltf", activations, encoder, preferred_element_type=jnp.float32
    )
    preact = lax.psum(partial_value, "layer") + bias[:, None, :]
    latent_act = (preact * masks).astype(jnp.bfloat16)
    rebuilt_list = []
    for target in range(LAYERS):
        summed = jnp.dot(
            latent_act[0], decoder[pair_index(0, target)], preferred_element_type=jnp.float32
        )
        for source in range(1, target + 1):
            summed = summed + jnp.dot(
                latent_act[source],
                decoder[pair_index(source, target)],
                preferred_element_type=jnp.float32,
            )
        rebuilt_list.append(summed)
    rebuilt = jnp.stack(rebuilt_list)
    complete = lax.psum(rebuilt, "lat")
    errors = (complete - targets.astype(jnp.float32)).astype(jnp.bfloat16)
    by_tokens = (((0,), (0,)), ((), ()))
    by_width = (((1,), (1,)), ((), ()))
    grad_pairs = []
    for source in range(LAYERS):
        for target in range(source, LAYERS):
            grad_pairs.append(
                lax.dot_general(
                    latent_act[source],
                    errors[target],
                    by_tokens,
                    preferred_element_type=jnp.float32,
                ).astype(jnp.bfloat16)
            )
    grad_decoder = jnp.stack(grad_pairs)
    grad_list = []
    for source in range(LAYERS):
        summed = lax.dot_general(
            errors[source],
            decoder[pair_index(source, source)],
            by_width,
            preferred_element_type=jnp.float32,
        )
        for target in range(source + 1, LAYERS):
            summed = summed + lax.dot_general(
                errors[target],
                decoder[pair_index(source, target)],
                by_width,
                preferred_element_type=jnp.float32,
            )
        grad_list.append(summed)
    grad_partial = jnp.stack(grad_list)
    block_rows = tokens // lax.axis_size("layer")
    share_rows = lax.psum_scatter(grad_partial, "layer", scatter_dimension=1, tiled=True)
    mask_rows = lax.dynamic_slice_in_dim(masks, lax.axis_index("layer") * block_rows, block_rows, 1)
    grad_pre = lax.all_gather(
        (share_rows * mask_rows).astype(jnp.bfloat16), "layer", axis=1, tiled=True
    )
    grad_encoder = jnp.einsum(
        "ltd,ltf->ldf", activations, grad_pre, preferred_element_type=jnp.float32
    ).astype(jnp.bfloat16)
    grad_bias = jnp.sum(grad_pre.astype(jnp.float32), axis=1)
    return (grad_encoder, grad_bias, grad_decoder)


def solution(mesh):
    placed = (
        P(None, None, "layer"),
        P(None, None, "layer"),
        P(None, "layer", "lat"),
        P(None, "lat"),
        P(None, "lat", "layer"),
        P(),
    )
    return jax.shard_map(
        on_device,
        mesh=mesh,
        in_specs=placed,
        out_specs=(P(None, "layer", "lat"), P(None, "lat"), P(None, "lat", "layer")),
        check_vma=False,
    )
```

profile of v0, /device:TPU:0, one launch (start us, length us, event | category | flops | bytes accessed | tf_op | source)
XLA Modules:
  0.0 1017.3 jit_solution(10485353639587241992)
XLA Ops:
  7.2 15.4 %fusion.266 = f32[8,512,1024]{2,1,0:T(8,128)} fusion(bf16[8,512,512]{2,1,0:T(8,128)(2,1)} %param.6, bf16[8,512,1024]{2,1,0:T(8,128)(2,1)} %param.8), kind=kOutput, calls=%fused_computation.385 | convolution fusion | flops 4294967296 | bytes 29360128 | tf_op jit(solution)/shard_map/ltd,ldf->ltf/dot_general | solution.py:24
  25.0 192.2 %compare_reduce_fusion = (pred[512,1024]{1,0:T(8,128)(4,1)S(1)}, pred[512,1024]{1,0:T(8,128)(4,1)S(1)}, pred[512,1024]{1,0:T(8,128)(4,1)S(1)}, pred[512,1024]{1,...) fusion(s32[512,64]{1,0:T(8,128)S(1)} %copy.26, ...), kind=kLoop, calls=%fused_computation | loop fusion | flops 532676608 | bytes 5246976 | tf_op jit(solution)/shard_map/reduce_or | solution.py:20
  223.9 108.9 %all-reduce.3.cloned.1.call-done = f32[8,512,1024]{2,1,0:T(8,128)} async-done(((f32[8,512,1024]{2,1,0:T(8,128)}), f32[8,512,1024]{2,1,0:T(8,128)}) %all-reduce.3.cloned.1.call-update) | async-done | bytes 16777232 | tf_op jit(solution)/shard_map/psum | solution.py:27
  332.8 9.7 select_convert_fusion
  342.5 5.7 fusion.102
  409.9 13.2 %convolution_add_fusion.24 = f32[512,512]{1,0:T(8,128)} fusion(f32[512,512]{1,0:T(8,128)S(1)} %fusion.172, bf16[36,1024,512]{2,1,0:T(8,128)(2,1)S(1)} %bitcast.587, bf16[8,512,1024]{2,1,0:T(8,128)(2,1)S(1)} %select_convert_fusion), kind=kOutput, calls=%fused_computation.99 | convolution fusion | flops 537133056 | bytes 4194304 | tf_op jit(solution)/shard_map/dot_general | solution.py:35
  443.3 176.7 %all-reduce.5.cloned.1.call-done = f32[8,512,512]{2,1,0:T(8,128)} async-done(((f32[8,512,512]{2,1,0:T(8,128)}), f32[8,512,512]{2,1,0:T(8,128)}) %all-reduce.5.cloned.1.call-update) | async-done | bytes 8388624 | tf_op jit(solution)/shard_map/psum | solution.py:42
  619.9 6.0 subtract_convert_fusion
  636.6 3.3 fusion.187
  639.9 3.3 fusion.191
  643.3 3.3 fusion.119
  649.8 3.3 fusion.154
  653.1 3.3 fusion.167
  656.4 3.3 fusion.177
  659.7 3.3 fusion.184
  672.9 3.3 fusion.113
  679.5 3.3 fusion.148
  682.8 3.7 fusion.161
  692.4 3.3 fusion.107
  699.0 3.3 fusion.104
  702.3 5.1 bitcast_dynamic-update-slice_fusion.7
  707.4 7.2 bitcast_dynamic-update-slice_fusion.6
  714.7 3.7 bitcast_dynamic-update-slice_fusion.5
  719.2 3.7 bitcast_dynamic-update-slice_fusion.4
  723.0 3.5 bitcast_dynamic-update-slice_fusion.3
  726.5 3.3 bitcast_dynamic-update-slice_fusion.2
  736.6 153.8 %reduce-scatter.2.cloned.1.call-done = f32[8,128,1024]{2,1,0:T(8,128)} async-done(((f32[8,512,1024]{2,1,0:T(8,128)}), f32[8,128,1024]{2,1,0:T(8,128)}) %reduce-scatter.2.cloned.1.call-update) | async-done | bytes 4194320 | tf_op jit(solution)/shard_map/reduce_scatter | solution.py:76
  890.4 4.6 multiply_convert_fusion
  964.1 18.5 %all-gather.2.cloned.1.call-done = bf16[8,512,1024]{2,1,0:T(8,128)(2,1)} async-done(((bf16[8,128,1024]{2,1,0:T(8,128)(2,1)}), bf16[8,512,1024]{2,1,0:T(8,128)(2,1)}) %all-gather.2.cloned.1.call-update) | async-done | bytes 8388624 | tf_op jit(solution)/shard_map/all_gather | solution.py:78
  982.6 10.5 %convert_bitcast_fusion = bf16[8,512,1024]{1,2,0:T(8,128)(2,1)} fusion(bf16[8,512,1024]{2,1,0:T(8,128)(2,1)} %all-gather.2.cloned.1.call-done, bf16[8,512,512]{2,1,0:T(8,128)(2,1)} %param.6), kind=kOutput, calls=%fused_computation.10 | convolution fusion | flops 4299161600 | bytes 20971520 | tf_op jit(solution)/shard_map/ltd,ltf->ldf/dot_general | solution.py:81
  993.1 11.4 %copy.28 = bf16[8,512,1024]{2,1,0:T(8,128)(2,1)} copy(bf16[8,512,1024]{1,2,0:T(8,128)(2,1)} %convert_bitcast_fusion) | data formatting | bytes 16777216
  1004.4 5.9 convert_reduce_fusion
  (166 shorter events, 203.6 us)
Async XLA Ops:
  7.2 325.6 %all-reduce.3.cloned.1.call-start = ((), (), s32[]{:S(2)}) async-start(), calls=%async_computation.1 | async-start | bytes 33554432 | tf_op jit(solution)/shard_map/psum | solution.py:27
  22.6 1.2 copy-start.10
  22.6 597.4 %all-reduce.5.cloned.1.call-start = ((), (), s32[]{:S(2)}) async-start(), calls=%async_computation.2 | async-start | bytes 16777216 | tf_op jit(solution)/shard_map/psum | solution.py:42
  24.3 308.5 %copy-start.11 = (f32[8,1024]{1,0:T(8,128)S(1)}, f32[8,1024]{1,0:T(8,128)}, u32[]{:S(2)}) copy-start(f32[8,1024]{1,0:T(8,128)} %param.9) | copy-start | bytes 98308
  332.8 38.9 %slice-start = ((s8[37748736]{0:T(1024)(128)(4,1)}), s8[4194304]{0:T(1024)(128)(4,1)S(1)}, s32[]{:S(2)}) async-start(s8[37748736]{0:T(1024)(128)(4,1)} %bitcast.586), calls=%async_computation.5 | async-start | bytes 8388608
  332.8 38.9 %slice-start.1 = ((s8[37748736]{0:T(1024)(128)(4,1)}), s8[4194304]{0:T(1024)(128)(4,1)S(1)}, s32[]{:S(2)}) async-start(s8[37748736]{0:T(1024)(128)(4,1)} %bitcast.586), calls=%async_computation.6 | async-start | bytes 8388608
  332.8 38.9 %slice-start.2 = ((s8[37748736]{0:T(1024)(128)(4,1)}), s8[4194304]{0:T(1024)(128)(4,1)S(1)}, s32[]{:S(2)}) async-start(s8[37748736]{0:T(1024)(128)(4,1)} %bitcast.586), calls=%async_computation.7 | async-start | bytes 8388608
  332.8 38.9 %slice-start.3 = ((s8[37748736]{0:T(1024)(128)(4,1)}), s8[4194304]{0:T(1024)(128)(4,1)S(1)}, s32[]{:S(2)}) async-start(s8[37748736]{0:T(1024)(128)(4,1)} %bitcast.586), calls=%async_computation.8 | async-start | bytes 8388608
  342.5 99.0 %copy-start.9 = (bf16[8,512,1024]{2,1,0:T(8,128)(2,1)}, bf16[8,512,1024]{2,1,0:T(8,128)(2,1)S(1)}, u32[]{:S(2)}) copy-start(bf16[8,512,1024]{2,1,0:T(8,128)(2,1)S(1)} %select_convert_fusion) | copy-start | bytes 25165828
  342.5 29.2 %slice-start.4 = ((s8[37748736]{0:T(1024)(128)(4,1)}), s8[4194304]{0:T(1024)(128)(4,1)S(1)}, s32[]{:S(2)}) async-start(s8[37748736]{0:T(1024)(128)(4,1)} %bitcast.586), calls=%async_computation.9 | async-start | bytes 8388608
  350.3 21.4 %slice-start.5 = ((s8[37748736]{0:T(1024)(128)(4,1)}), s8[4194304]{0:T(1024)(128)(4,1)S(1)}, s32[]{:S(2)}) async-start(s8[37748736]{0:T(1024)(128)(4,1)} %bitcast.586), calls=%async_computation.10 | async-start | bytes 8388608
  356.4 15.4 %slice-start.6 = ((s8[37748736]{0:T(1024)(128)(4,1)}), s8[4194304]{0:T(1024)(128)(4,1)S(1)}, s32[]{:S(2)}) async-start(s8[37748736]{0:T(1024)(128)(4,1)} %bitcast.586), calls=%async_computation.11 | async-start | bytes 8388608
  360.4 11.4 %slice-start.7 = ((s8[37748736]{0:T(1024)(128)(4,1)}), s8[4194304]{0:T(1024)(128)(4,1)S(1)}, s32[]{:S(2)}) async-start(s8[37748736]{0:T(1024)(128)(4,1)} %bitcast.586), calls=%async_computation.12 | async-start | bytes 8388608
  366.4 5.4 slice-start.8
  426.0 10.5 %copy-start.13 = (f32[512,512]{1,0:T(8,128)S(1)}, f32[512,512]{1,0:T(8,128)}, u32[]{:S(2)}) copy-start(f32[512,512]{1,0:T(8,128)} %convolution_add_fusion.19) | copy-start | bytes 3145732
  427.7 10.5 %copy-start.12 = (f32[512,512]{1,0:T(8,128)S(1)}, f32[512,512]{1,0:T(8,128)}, u32[]{:S(2)}) copy-start(f32[512,512]{1,0:T(8,128)} %convolution_add_fusion.14) | copy-start | bytes 3145732
  443.2 447.2 %reduce-scatter.2.cloned.1.call-start = ((), (), s32[]{:S(2)}) async-start(), calls=%async_computation.3 | async-start | bytes 20971520 | tf_op jit(solution)/shard_map/reduce_scatter | solution.py:76
  626.0 107.1 %copy-start = (bf16[8,512,512]{2,1,0:T(8,128)(2,1)}, bf16[8,512,512]{2,1,0:T(8,128)(2,1)S(1)}, u32[]{:S(2)}) copy-start(bf16[8,512,512]{2,1,0:T(8,128)(2,1)S(1)} %subtract_convert_fusion) | copy-start | bytes 12582916
  714.7 3.7 copy-start.5
  714.7 3.7 copy-start.6
  714.7 3.7 copy-start.7
  714.7 4.5 copy-start.8
  719.2 7.2 copy-start.3
  719.2 7.2 copy-start.4
  723.0 6.8 copy-start.2
  736.4 246.2 %all-gather.2.cloned.1.call-start = ((), (), s32[]{:S(2)}) async-start(), calls=%async_computation.4 | async-start | bytes 10485760 | tf_op jit(solution)/shard_map/all_gather | solution.py:78
  895.0 6.5 copy-start.1
  898.2 12.4 %slice-start.9 = ((s8[8388608]{0:T(1024)(128)(4,1)}), s8[4194304]{0:T(1024)(128)(4,1)S(1)}, s32[]{:S(2)}) async-start(s8[8388608]{0:T(1024)(128)(4,1)} %bitcast.588), calls=%async_computation.14 | async-start | bytes 8388608
  904.5 6.1 slice-start.10
Sparse Core Ops, SparseCore 0:
  22.7 310.0 all-reduce.2
  443.3 176.5 all-reduce.4
  736.5 153.8 reduce-scatter.1
  895.1 87.4 all-gather.1
where the time goes:
time: 1030 us; the launch traced here: 1020 us
  waiting for transfers between devices  458 us (44%)
  matrix products  305 us (30%)
  other arithmetic  218 us (21%)
  local copies, waits for them, and re-layouts  21.2 us (2%)
  between operations  14.7 us (1%)
    reduce_or x1, other arithmetic, on_device(): jnp.any(active[source][:, :, None] == columns[None, None, :], axis=1)  192 us
    psum x1, waiting for transfers between devices, on_device(): complete = lax.psum(rebuilt, 'lat')  177 us
    reduce_scatter x1, waiting for transfers between devices, on_device(): lax.psum_scatter(grad_partial, 'layer', scatter_dimension=1, tiled=True)  154 us
    psum x1, waiting for transfers between devices, on_device(): preact = lax.psum(partial_value, 'layer') + bias[:, None, :]  109 us
    dot_general x28, matrix products, on_device(): lax.dot_general(errors[target], decoder[pair_index(source, target)], by_w...  85.2 us
    dot_general x28, matrix products, on_device(): jnp.dot(latent_act[source], decoder[pair_index(source, target)], preferre...  76.7 us
    dot_general x36, matrix products, on_device(): lax.dot_general(latent_act[source], errors[target], by_tokens, preferred_...  69.1 us
    dot_general x8, matrix products, on_device(): lax.dot_general(errors[source], decoder[pair_index(source, source)], by_w...  24.2 us
  transfers between devices with their start and end apart: 4, of which 4 were waited for; matrix products, arithmetic and copies ran while one was open for 26% of the time, Pallas kernels for 0%

commit v1 on v0

v1 whole, which is shorter than its diff:
```python
import functools

import jax
import jax.numpy as jnp
import numpy as np
from jax import lax
from jax.experimental import pallas as pl
from jax.experimental.pallas import tpu as pltpu
from jax.sharding import PartitionSpec as P

LANES = 128
FIELD = 7
PER_WORD = 4
GROUPS = ((7, 6), (5, 4), (3, 2, 1, 0))


def pair_index(source, target, layers):
    return source * layers - source * (source - 1) // 2 + (target - source)


def params(**kw):
    return pltpu.CompilerParams(vmem_limit_bytes=60 * 1024 * 1024, **kw)


def cost(flops, moved):
    return pl.CostEstimate(flops=int(flops), bytes_accessed=int(moved), transcendentals=0)


def pick(dense_block, index):
    lane = index & (LANES - 1)
    block = index >> 7
    value = jnp.zeros(index.shape, jnp.float32)
    for b in range(dense_block.shape[1] // LANES):
        part = dense_block[:, b * LANES : (b + 1) * LANES]
        got = jnp.take_along_axis(part, lane, axis=1, mode="promise_in_bounds")
        value = jnp.where(block == b, got, value)
    return value


def store_half(out_ref, rows, value, odd):
    half = lax.broadcasted_iota(jnp.int32, value.shape, 1) // (LANES // 2)
    mine = half == odd

    @pl.when(odd == 0)
    def _():
        out_ref[0, rows, :] = jnp.where(mine, value, 0.0)

    @pl.when(odd == 1)
    def _():
        out_ref[0, rows, :] = jnp.where(mine, value, out_ref[0, rows, :])


def encode_kernel(act_ref, enc_ref, bias_ref, index_ref, out_ref):
    odd = pl.program_id(0) % 2
    step = 128

    @pl.loop(0, act_ref.shape[1] // step)
    def _(i):
        rows = pl.ds(pl.multiple_of(i * step, step), step)
        pre = jnp.dot(act_ref[0, rows, :], enc_ref[0], preferred_element_type=jnp.float32)
        pre = pre + bias_ref[0]
        store_half(out_ref, rows, pick(pre, index_ref[0, rows, :]), odd)


def encode(act, enc, bias, index2):
    layers, tokens, width = act.shape
    lat = enc.shape[2]
    return pl.pallas_call(
        encode_kernel,
        grid=(layers,),
        in_specs=[
            pl.BlockSpec((1, tokens, width), lambda l: (l, 0, 0)),
            pl.BlockSpec((1, width, lat), lambda l: (l, 0, 0)),
            pl.BlockSpec((1, 1, lat), lambda l: (l, 0, 0)),
            pl.BlockSpec((1, tokens, LANES), lambda l: (l // 2, 0, 0)),
        ],
        out_specs=pl.BlockSpec((1, tokens, LANES), lambda l: (l // 2, 0, 0)),
        out_shape=jax.ShapeDtypeStruct((layers // 2, tokens, LANES), jnp.float32),
        compiler_params=params(),
        cost_estimate=cost(2 * layers * tokens * width * lat, act.size * 2 + enc.size * 2),
        name="encode",
    )(act, enc, bias[:, None, :], index2)


def compact_kernel(dense_ref, index_ref, out_ref):
    odd = pl.program_id(0) % 2
    step = 64

    @pl.loop(0, dense_ref.shape[1] // step)
    def _(i):
        rows = pl.ds(pl.multiple_of(i * step, step), step)
        store_half(out_ref, rows, pick(dense_ref[0, rows, :], index_ref[0, rows, :]), odd)


def compact(dense, index2):
    layers, tokens, lat = dense.shape
    return pl.pallas_call(
        compact_kernel,
        grid=(layers,),
        in_specs=[
            pl.BlockSpec((1, tokens, lat), lambda l: (l, 0, 0)),
            pl.BlockSpec((1, tokens, LANES), lambda l: (l // 2, 0, 0)),
        ],
        out_specs=pl.BlockSpec((1, tokens, LANES), lambda l: (l // 2, 0, 0)),
        out_shape=jax.ShapeDtypeStruct((layers // 2, tokens, LANES), jnp.float32),
        compiler_params=params(),
        cost_estimate=cost(0, dense.size * 4),
        name="compact",
    )(dense, index2)


def slots_kernel(words, blocks, index_ref, out_ref, *scratch):
    row_ref, code_refs = scratch[0], scratch[1:]
    tokens = index_ref.shape[2]
    slots = index_ref.shape[1]

    @pl.loop(0, tokens // LANES)
    def _(c):
        cols = pl.ds(pl.multiple_of(c * LANES, LANES), LANES)
        index = index_ref[0, :, cols]
        block = index >> 7
        local = (index >= 0) & (block < blocks)
        row_ref[...] = jnp.where(local, index & (LANES - 1), -1)
        code = (lax.broadcasted_iota(jnp.int32, index.shape, 0) + 1) << (FIELD * (block & (PER_WORD - 1)))
        for w in range(words):
            code_refs[w][...] = jnp.where((block >> 2) == w, code, 0)
        rows = lax.broadcasted_iota(jnp.int32, (LANES, LANES), 0)
        totals = [jnp.zeros((LANES, LANES), jnp.int32) for _ in range(words)]
        for k in range(slots):
            same = row_ref[k : k + 1, :] == rows
            for w in range(words):
                totals[w] = totals[w] | jnp.where(same, code_refs[w][k : k + 1, :], 0)
        for w in range(words):
            out_ref[0, w, cols, :] = totals[w].T


def slot_table(index_t, lat):
    layers, slots, tokens = index_t.shape
    blocks = lat // LANES
    words = -(-blocks // PER_WORD)
    return pl.pallas_call(
        functools.partial(slots_kernel, words, blocks),
        grid=(layers,),
        in_specs=[pl.BlockSpec((1, slots, tokens), lambda l: (l, 0, 0))],
        out_specs=pl.BlockSpec((1, words, tokens, LANES), lambda l: (l, 0, 0, 0)),
        out_shape=jax.ShapeDtypeStruct((layers, words, tokens, LANES), jnp.int32),
        scratch_shapes=[pltpu.VMEM((slots, LANES), jnp.int32)] * (1 + words),
        compiler_params=params(),
        cost_estimate=cost(2e10, 1e6),
        name="slot_table",
    )(index_t)


def spread(packed_ref, table_ref, rows, b, odd):
    field = (table_ref[0, b // PER_WORD, rows, :] >> (FIELD * (b % PER_WORD))) & (2**FIELD - 1)
    lane = jnp.maximum(field - 1, 0) + odd * (LANES // 2)
    packed = packed_ref[0, rows, :].astype(jnp.float32)
    got = jnp.take_along_axis(packed, lane, axis=1, mode="promise_in_bounds")
    return jnp.where(field > 0, got, 0.0)


def expand_kernel(packed_ref, table_ref, out_ref, flipped_ref):
    odd = pl.program_id(0) % 2
    tokens = packed_ref.shape[1]

    @pl.loop(0, tokens // LANES)
    def _(i):
        rows = pl.ds(pl.multiple_of(i * LANES, LANES), LANES)
        for b in range(out_ref.shape[2] // LANES):
            value = spread(packed_ref, table_ref, rows, b, odd)
            cols = slice(b * LANES, (b + 1) * LANES)
            out_ref[0, rows, cols] = value.astype(jnp.bfloat16)
            flipped_ref[0, cols, rows] = value.T.astype(jnp.bfloat16)


def expand(packed, table, lat):
    layers, words, tokens, _ = table.shape
    return pl.pallas_call(
        expand_kernel,
        grid=(layers,),
        in_specs=[
            pl.BlockSpec((1, tokens, LANES), lambda l: (l // 2, 0, 0)),
            pl.BlockSpec((1, words, tokens, LANES), lambda l: (l, 0, 0, 0)),
        ],
        out_specs=[
            pl.BlockSpec((1, tokens, lat), lambda l: (l, 0, 0)),
            pl.BlockSpec((1, lat, tokens), lambda l: (l, 0, 0)),
        ],
        out_shape=[
            jax.ShapeDtypeStruct((layers, tokens, lat), jnp.bfloat16),
            jax.ShapeDtypeStruct((layers, lat, tokens), jnp.bfloat16),
        ],
        compiler_params=params(),
        cost_estimate=cost(0, 4 * layers * tokens * lat),
        name="expand",
    )(packed, table)


def encoder_grad_kernel(packed_ref, table_ref, act_ref, grad_ref, bias_ref, dense_ref):
    odd = pl.program_id(0) % 2
    tokens = packed_ref.shape[1]
    lat = dense_ref.shape[1]
    bias_ref[...] = jnp.zeros_like(bias_ref)

    @pl.loop(0, tokens // LANES)
    def _(i):
        rows = pl.ds(pl.multiple_of(i * LANES, LANES), LANES)
        for b in range(lat // LANES):
            value = spread(packed_ref, table_ref, rows, b, odd)
            cols = slice(b * LANES, (b + 1) * LANES)
            dense_ref[rows, cols] = value.astype(jnp.bfloat16)
            bias_ref[0, :, cols] += jnp.sum(value, axis=0, keepdims=True)

    step = 256

    @pl.loop(0, lat // step)
    def _(j):
        cols = pl.ds(pl.multiple_of(j * step, step), step)
        grad_ref[0, :, cols] = lax.dot_general(
            act_ref[0], dense_ref[:, cols], (((0,), (0,)), ((), ())), preferred_element_type=jnp.float32
        ).astype(jnp.bfloat16)


def encoder_grad(packed, table, act, lat):
    layers, words, tokens, _ = table.shape
    width = act.shape[2]
    return pl.pallas_call(
        encoder_grad_kernel,
        grid=(layers,),
        in_specs=[
            pl.BlockSpec((1, tokens, LANES), lambda l: (l // 2, 0, 0)),
            pl.BlockSpec((1, words, tokens, LANES), lambda l: (l, 0, 0, 0)),
            pl.BlockSpec((1, tokens, width), lambda l: (l, 0, 0)),
        ],
        out_specs=[
            pl.BlockSpec((1, width, lat), lambda l: (l, 0, 0)),
            pl.BlockSpec((1, 1, lat), lambda l: (l, 0, 0)),
        ],
        out_shape=[
            jax.ShapeDtypeStruct((layers, width, lat), jnp.bfloat16),
            jax.ShapeDtypeStruct((layers, 1, lat), jnp.float32),
        ],
        scratch_shapes=[pltpu.VMEM((tokens, lat), jnp.bfloat16)],
        compiler_params=params(),
        cost_estimate=cost(2 * layers * tokens * width * lat, 4 * layers * width * lat),
        name="encoder_grad",
    )(packed, table, act)


def group_tables(group, layers):
    rows = [
        (source, place, pair_index(source, target, layers), int(source == target))
        for source in range(max(group) + 1)
        for place, target in enumerate(group)
        if target >= source
    ]
    return np.array(rows, np.int32)


def decode_kernel(tab_ref, lat_ref, dec_ref, out_ref, total_ref):
    i = pl.program_id(0)
    source, place, last = tab_ref[i, 0], tab_ref[i, 1], tab_ref[i, 3]
    step = 256

    @pl.loop(0, dec_ref.shape[2] // step)
    def _(j):
        cols = pl.ds(pl.multiple_of(j * step, step), step)
        part = jnp.dot(lat_ref[0], dec_ref[0, :, cols], preferred_element_type=jnp.float32)

        @pl.when(source == 0)
        def _():
            total_ref[place, :, cols] = part

        @pl.when(source > 0)
        def _():
            total_ref[place, :, cols] += part

    @pl.when(last == 1)
    def _():
        out_ref[place] = total_ref[place].astype(jnp.bfloat16)


def decode(group, lats, decoder):
    layers, tokens, lat = lats.shape
    width = decoder.shape[2]
    tab = group_tables(group, layers)
    shape = (len(group), tokens, width)
    return pl.pallas_call(
        decode_kernel,
        grid_spec=pltpu.PrefetchScalarGridSpec(
            num_scalar_prefetch=1,
            grid=(len(tab),),
            in_specs=[
                pl.BlockSpec((1, tokens, lat), lambda i, t: (t[i, 0], 0, 0)),
                pl.BlockSpec((1, lat, width), lambda i, t: (t[i, 2], 0, 0)),
            ],
            out_specs=pl.BlockSpec(shape, lambda i, t: (0, 0, 0)),
            scratch_shapes=[pltpu.VMEM(shape, jnp.float32)],
        ),
        out_shape=jax.ShapeDtypeStruct(shape, jnp.bfloat16),
        compiler_params=params(),
        cost_estimate=cost(2 * len(tab) * tokens * lat * width, 3 * len(tab) * lat * width),
        name="decode",
    )(jnp.asarray(tab), lats, decoder)


def backward_kernel(first_group, tab_ref, err_ref, flipped_ref, dec_ref, *rest):
    if first_group:
        act_ref, grad_ref = rest
    else:
        before_ref, _, act_ref, grad_ref = rest
    i = pl.program_id(0)
    place, fresh = tab_ref[i, 1], tab_ref[i, 4]
    step = 256

    @pl.loop(0, dec_ref.shape[1] // step)
    def _(j):
        cols = pl.ds(pl.multiple_of(j * step, step), step)
        grad_ref[0, cols, :] = jnp.dot(
            flipped_ref[0, cols, :], err_ref[place], preferred_element_type=jnp.float32
        ).astype(jnp.bfloat16)
        part = lax.dot_general(
            err_ref[place], dec_ref[0, cols, :], (((1,), (1,)), ((), ())), preferred_element_type=jnp.float32
        )

        @pl.when(fresh == 1)
        def _():
            act_ref[0, :, cols] = part if first_group else part + before_ref[0, :, cols]

        @pl.when(fresh == 0)
        def _():
            act_ref[0, :, cols] += part


def backward(group, errors, flipped, decoder, before, grads):
    layers, lat, tokens = flipped.shape
    pairs, _, width = decoder.shape
    tab = group_tables(group, layers)
    fresh = np.concatenate([[1], (np.diff(tab[:, 0]) != 0).astype(np.int32)])[:, None]
    tab = np.concatenate([tab, fresh], axis=1).astype(np.int32)
    act_spec = pl.BlockSpec((1, tokens, lat), lambda i, t: (t[i, 0], 0, 0))
    pair_spec = pl.BlockSpec((1, lat, width), lambda i, t: (t[i, 2], 0, 0))
    first = before is None
    in_specs = [
        pl.BlockSpec(errors.shape, lambda i, t: (0, 0, 0)),
        pl.BlockSpec((1, lat, tokens), lambda i, t: (t[i, 0], 0, 0)),
        pair_spec,
    ]
    operands = [jnp.asarray(tab), errors, flipped, decoder]
    if not first:
        in_specs += [act_spec, pl.BlockSpec(memory_space=pl.ANY)]
        operands += [before, grads]
    return pl.pallas_call(
        functools.partial(backward_kernel, first),
        grid_spec=pltpu.PrefetchScalarGridSpec(
            num_scalar_prefetch=1,
            grid=(len(tab),),
            in_specs=in_specs,
            out_specs=[act_spec, pair_spec],
        ),
        out_shape=[
            jax.ShapeDtypeStruct((layers, tokens, lat), jnp.float32),
            jax.ShapeDtypeStruct((pairs, lat, width), jnp.bfloat16),
        ],
        input_output_aliases={} if first else {4: 0, 5: 1},
        compiler_params=params(),
        cost_estimate=cost(4 * len(tab) * tokens * lat * width, 8 * len(tab) * lat * width),
        name="backward",
    )(*operands)


def exchange(packed):
    shape = packed.shape
    rows = packed.reshape((-1, shape[-1]))
    share = lax.psum_scatter(rows, "layer", scatter_dimension=0, tiled=True)
    return lax.all_gather(share.astype(jnp.bfloat16), "layer", axis=0, tiled=True).reshape(shape)


def on_device(activations, targets, encoder, bias, decoder, active):
    layers, tokens, slots = active.shape
    lat = encoder.shape[2]
    index = active - lax.axis_index("lat") * lat
    index2 = index.reshape((layers // 2, 2, tokens, slots)).transpose((0, 2, 1, 3))
    index2 = index2.reshape((layers // 2, tokens, 2 * slots))
    index_t = jnp.swapaxes(index, 1, 2)
    once = jnp.where(lax.axis_index("layer") == 0, bias, 0.0)
    packed = exchange(encode(activations, encoder, once, index2))
    table = slot_table(index_t, lat)
    lats, flipped = expand(packed, table, lat)
    groups = [tuple(m for m in group if m < layers) for group in GROUPS]
    summed = []
    for group in groups:
        partial = decode(group, lats, decoder)
        if summed:
            partial, summed[-1] = lax.optimization_barrier((partial, summed[-1]))
        summed.append(lax.psum(partial, "lat"))
    act = grads = None
    for group, complete in zip(groups, summed):
        wanted = jnp.stack([targets[m] for m in group])
        errors = (complete.astype(jnp.float32) - wanted.astype(jnp.float32)).astype(jnp.bfloat16)
        act, grads = backward(group, errors, flipped, decoder, act, grads)
    packed_grad = exchange(compact(act, index2))
    grad_encoder, grad_bias = encoder_grad(packed_grad, table, activations, lat)
    return (grad_encoder, grad_bias[:, 0, :], grads)


def solution(mesh):
    placed = (
        P(None, None, "layer"),
        P(None, None, "layer"),
        P(None, "layer", "lat"),
        P(None, "lat"),
        P(None, "lat", "layer"),
        P(),
    )
    return jax.shard_map(
        on_device,
        mesh=mesh,
        in_specs=placed,
        out_specs=(P(None, "layer", "lat"), P(None, "lat"), P(None, "lat", "layer")),
        check_vma=False,
    )
```

time: 1030 us -> 445 us (0.43); the launches traced: 1020 us -> 444 us
  waiting for transfers between devices: 458 us -> 111 us
  matrix products: 305 us -> 0 us
  Pallas kernels: 0 us -> 276 us
  other arithmetic: 218 us -> 13.6 us
  blocking collectives: 0 us -> 22.1 us
  local copies, waits for them, and re-layouts: 21.2 us -> 7.07 us
    dot_general x110 -> x0, matrix products: 305 us -> none  [the longest x28 85.2 us: on_device(): lax.dot_general(errors[target], decoder[pair_index(source, target)], by_w...]
    pallas_call x0 -> x11, Pallas kernels: none -> 276 us  [the longest x3 93.9 us: backward(): pl.pallas_call(functools.partial(backward_kernel, first), grid_spec=pltpu...]
    psum x2 -> x3, waiting for transfers between devices: 286 us -> 83 us  [on_device(): summed.append(lax.psum(partial, 'lat'))]
    reduce_or x1 -> x0, other arithmetic: 192 us -> none  [on_device(): jnp.any(active[source][:, :, None] == columns[None, None, :], axis=1)]
    reduce_scatter x1 -> x2, waiting for transfers between devices: 154 us -> 27.7 us  [exchange(): share = lax.psum_scatter(rows, 'layer', scatter_dimension=0, tiled=True)]
    all_gather x0 -> x2, blocking collectives: none -> 22.1 us  [exchange(): lax.all_gather(share.astype(jnp.bfloat16), 'layer', axis=0, tiled=True)]
    all_gather x1 -> x0, waiting for transfers between devices: 18.5 us -> none  [on_device(): lax.all_gather((share_rows * mask_rows).astype(jnp.bfloat16), 'layer', ax...]
    unnamed x58 -> x11, local copies, waits for them, and re-layouts: 19.3 us -> 1.4 us
  transfers between devices with their start and end apart: 4 -> 5, of which waited for: 4 -> 4; matrix products, arithmetic and copies ran while one was open for 26% -> 2% of each run, Pallas kernels for 0% -> 31%
where the time goes in v1:
time: 445 us; the launch traced here: 444 us
  Pallas kernels  276 us (62%)
  waiting for transfers between devices  111 us (25%)
  blocking collectives  22.1 us (5%)
  between operations  13.8 us (3%)
  other arithmetic  13.6 us (3%)
  local copies, waits for them, and re-layouts  7.07 us (2%)
    pallas_call x3, Pallas kernels, backward(): pl.pallas_call(functools.partial(backward_kernel, first), grid_spec=pltpu...  93.9 us
    psum x3, waiting for transfers between devices, on_device(): summed.append(lax.psum(partial, 'lat'))  83 us
    pallas_call x3, Pallas kernels, decode(): pl.pallas_call(decode_kernel, grid_spec=pltpu.PrefetchScalarGridSpec(num_...  55 us
    pallas_call x1, Pallas kernels, slot_table(): pl.pallas_call(functools.partial(slots_kernel, words, blocks), grid=(laye...  39.8 us
    pallas_call x1, Pallas kernels, encoder_grad(): pl.pallas_call(encoder_grad_kernel, grid=(layers,), in_specs=[pl.BlockSpe...  28.2 us
    reduce_scatter x2, waiting for transfers between devices, exchange(): share = lax.psum_scatter(rows, 'layer', scatter_dimension=0, tiled=True)  27.7 us
    all_gather x2, blocking collectives, exchange(): lax.all_gather(share.astype(jnp.bfloat16), 'layer', axis=0, tiled=True)  22.1 us
    pallas_call x1, Pallas kernels, expand(): pl.pallas_call(expand_kernel, grid=(layers,), in_specs=[pl.BlockSpec((1,...  21.1 us
  transfers between devices with their start and end apart: 5, of which 4 were waited for; matrix products, arithmetic and copies ran while one was open for 2% of the time, Pallas kernels for 31%

profile of v1, /device:TPU:0, one launch (start us, length us, event | category | flops | bytes accessed | tf_op | source)
XLA Modules:
  0.0 443.7 jit_solution(1983214200294820433)
XLA Ops:
  7.2 0.8 broadcast_select_fusion
  8.0 0.6 broadcast_in_dim.8.bias_ref
  8.6 1.3 broadcast_subtract_fusion
  10.0 1.3 copy.20.index_ref
  11.3 19.7 %encode.1 = f32[4,512,128]{2,1,0:T(8,128)} custom-call(bf16[8,512,512]{2,1,0:T(8,128)(2,1)} %act_ref.3, bf16[8,512,1024]{2,1,0:T(8,128)(2,1)} %enc_ref.1, f32[8,1,1024]{2,1,0:T(1,128)} %broadcast_in_dim.8.bias_ref, s32[4,512,128]{2,1,0:T(8,128)} %copy.20.index_ref), custom_call_target="tpu_custom_call" | custom-call | flops 4294967296 | bytes 12582912 | tf_op jit(solution)/shard_map/encode/pallas_call | solution.py:68
  31.1 0.0 all-reduce.4.cloned.1.call-start
  31.1 3.7 fusion
  34.8 1.1 fusion.1.index_ref
  35.9 39.8 %slot_table.1.table_ref = s32[8,2,512,128]{3,2,1,0:T(8,128)} custom-call(s32[8,64,512]{2,1,0:T(8,128)} %fusion.1.index_ref), custom_call_target="tpu_custom_call" | custom-call | flops 20000000000 | bytes 1000000 | tf_op jit(solution)/shard_map/slot_table/pallas_call | solution.py:141
  75.7 1.0 convert_element_type.33
  76.6 11.5 %all_gather.6 = bf16[2048,128]{1,0:T(8,128)(2,1)} all-gather(bf16[512,128]{1,0:T(8,128)(2,1)S(1)} %convert_element_type.33), channel_id=1, replica_groups=mesh['layer'=4,'lat'=8] {'layer'}, dimensions={0}, use_global_device_ids=true | all-gather | bytes 655360 | tf_op jit(solution)/shard_map/all_gather | solution.py:376
  88.1 21.1 %expand.1 = (bf16[8,512,1024]{2,1,0:T(8,128)(2,1)}, bf16[8,1024,512]{2,1,0:T(8,128)(2,1)}) custom-call(bf16[4,512,128]{2,1,0:T(8,128)(2,1)} %bitcast.16, s32[8,2,512,128]{3,2,1,0:T(8,128)} %slot_table.1.table_ref), custom_call_target="tpu_custom_call" | custom-call | bytes 16777216 | tf_op jit(solution)/shard_map/expand/pallas_call | solution.py:178
  109.2 22.2 %decode.5 = bf16[2,512,512]{2,1,0:T(8,128)(2,1)} custom-call(s32[15,4]{1,0:T(8,128)} %constant.26.clone.tab_ref, bf16[8,512,1024]{2,1,0:T(8,128)(2,1)} %get-tuple-element.17.lat_ref, bf16[36,1024,512]{2,1,0:T(8,128)(2,1)} %dec_ref.11), custom_call_target="tpu_custom_call" | custom-call | flops 8053063680 | bytes 23592960 | tf_op jit(solution)/shard_map/decode/pallas_call | solution.py:288
  131.4 0.0 all-reduce.6.cloned.1.call-start
  131.4 17.1 %decode.4 = bf16[2,512,512]{2,1,0:T(8,128)(2,1)} custom-call(s32[11,4]{1,0:T(8,128)} %constant.27.clone.tab_ref, bf16[8,512,1024]{2,1,0:T(8,128)(2,1)} %get-tuple-element.17.lat_ref, bf16[36,1024,512]{2,1,0:T(8,128)(2,1)} %dec_ref.11), custom_call_target="tpu_custom_call" | custom-call | flops 5905580032 | bytes 17301504 | tf_op jit(solution)/shard_map/decode/pallas_call | solution.py:288
  148.5 15.8 %decode.3 = bf16[4,512,512]{2,1,0:T(8,128)(2,1)} custom-call(s32[10,4]{1,0:T(8,128)} %constant.28.clone.tab_ref, bf16[8,512,1024]{2,1,0:T(8,128)(2,1)} %get-tuple-element.17.lat_ref, bf16[36,1024,512]{2,1,0:T(8,128)(2,1)} %dec_ref.11), custom_call_target="tpu_custom_call" | custom-call | flops 5368709120 | bytes 15728640 | tf_op jit(solution)/shard_map/decode/pallas_call | solution.py:288
  164.3 26.8 %all-reduce.4.cloned.1.call-done = bf16[2,512,512]{2,1,0:T(8,128)(2,1)} async-done(((bf16[2,512,512]{2,1,0:T(8,128)(2,1)}), bf16[2,512,512]{2,1,0:T(8,128)(2,1)}) %all-reduce.4.cloned.1.call-update) | async-done | bytes 1048592 | tf_op jit(solution)/shard_map/psum | solution.py:396
  191.2 2.5 subtract_convert_fusion.1.err_ref
  193.7 35.1 %backward.3 = (f32[8,512,1024]{2,1,0:T(8,128)}, bf16[36,1024,512]{2,1,0:T(8,128)(2,1)}) custom-call(s32[15,5]{1,0:T(8,128)} %constant.29.clone.tab_ref, bf16[2,512,512]{2,1,0:T(8,128)(2,1)} %subtract_convert_fusion.1.err_ref, bf16[8,1024,512]{2,1,0:T(8,128)(2,1)} %get-tuple-element.20.flipped_ref, bf16[36,1024,512]{2,1,0:T(8,128)(2,1)} %dec_ref.11), custom_call_target="tpu_custom_call" | custom-call | flops 16106127360 | bytes 62914560 | tf_op jit(solution)/shard_map/backward/pallas_call | solution.py:353
  228.8 23.0 %all-reduce.6.cloned.1.call-done = bf16[2,512,512]{2,1,0:T(8,128)(2,1)} async-done(((bf16[2,512,512]{2,1,0:T(8,128)(2,1)}), bf16[2,512,512]{2,1,0:T(8,128)(2,1)}) %all-reduce.6.cloned.1.call-update) | async-done | bytes 1048592 | tf_op jit(solution)/shard_map/psum | solution.py:396
  251.8 0.0 reduce-scatter.5.cloned.1.call-start
  251.9 2.5 subtract_convert_fusion.2.err_ref
  254.4 30.8 %backward.4 = (f32[8,512,1024]{2,1,0:T(8,128)}, bf16[36,1024,512]{2,1,0:T(8,128)(2,1)}) custom-call(s32[11,5]{1,0:T(8,128)} %constant.30.clone.tab_ref, bf16[2,512,512]{2,1,0:T(8,128)(2,1)} %subtract_convert_fusion.2.err_ref, bf16[8,1024,512]{2,1,0:T(8,128)(2,1)} %get-tuple-element.20.flipped_ref, ...), custom_call_target="tpu_custom_call", output_to_operand_aliasing={{0}: (4, {}), {1}: (5, {})} | custom-call | flops 11811160064 | bytes 46137344 | tf_op jit(solution)/shard_map/backward/pallas_call | solution.py:353
  285.2 33.2 %all-reduce.8.cloned.1.call-done = bf16[4,512,512]{2,1,0:T(8,128)(2,1)} async-done(((bf16[4,512,512]{2,1,0:T(8,128)(2,1)}), bf16[4,512,512]{2,1,0:T(8,128)(2,1)}) %all-reduce.8.cloned.1.call-update) | async-done | bytes 2097168 | tf_op jit(solution)/shard_map/psum | solution.py:396
  318.3 3.5 subtract_convert_fusion.err_ref
  321.8 28.1 %backward.5 = (f32[8,512,1024]{2,1,0:T(8,128)}, bf16[36,1024,512]{2,1,0:T(8,128)(2,1)}) custom-call(s32[10,5]{1,0:T(8,128)} %constant.31.clone.tab_ref, bf16[4,512,512]{2,1,0:T(8,128)(2,1)} %subtract_convert_fusion.err_ref, bf16[8,1024,512]{2,1,0:T(8,128)(2,1)} %get-tuple-element.20.flipped_ref, ...), custom_call_target="tpu_custom_call", output_to_operand_aliasing={{0}: (4, {}), {1}: (5, {})} | custom-call | flops 10737418240 | bytes 41943040 | tf_op jit(solution)/shard_map/backward/pallas_call | solution.py:353
  349.9 18.4 %compact.1 = f32[4,512,128]{2,1,0:T(8,128)} custom-call(f32[8,512,1024]{2,1,0:T(8,128)} %get-tuple-element.27.dense_ref, s32[4,512,128]{2,1,0:T(8,128)} %copy.20.index_ref), custom_call_target="tpu_custom_call" | custom-call | bytes 16777216 | tf_op jit(solution)/shard_map/compact/pallas_call | solution.py:97
  368.4 27.7 %reduce-scatter.5.cloned.1.call-done = f32[512,128]{1,0:T(8,128)} async-done(((f32[2048,128]{1,0:T(8,128)}), f32[512,128]{1,0:T(8,128)}) %reduce-scatter.5.cloned.1.call-update) | async-done | bytes 262160 | tf_op jit(solution)/shard_map/reduce_scatter | solution.py:375
  396.0 1.0 convert_element_type.43
  397.0 10.6 %all_gather.7 = bf16[2048,128]{1,0:T(8,128)(2,1)} all-gather(bf16[512,128]{1,0:T(8,128)(2,1)S(1)} %convert_element_type.43), channel_id=1, replica_groups=mesh['layer'=4,'lat'=8] {'layer'}, dimensions={0}, use_global_device_ids=true | all-gather | bytes 655360 | tf_op jit(solution)/shard_map/all_gather | solution.py:376
  407.6 28.2 %encoder_grad.1 = (bf16[8,512,1024]{2,1,0:T(8,128)(2,1)}, f32[8,1,1024]{2,1,0:T(1,128)}) custom-call(bf16[4,512,128]{2,1,0:T(8,128)(2,1)} %bitcast.18, s32[8,2,512,128]{3,2,1,0:T(8,128)} %slot_table.1.table_ref, bf16[8,512,512]{2,1,0:T(8,128)(2,1)} %act_ref.3), custom_call_target="tpu_custom_call" | custom-call | flops 4294967296 | bytes 16777216 | tf_op jit(solution)/shard_map/encoder_grad/pallas_call | solution.py:227
  435.8 1.4 copy.24
  (18 shorter events, 0.2 us)
Async XLA Ops:
  7.2 68.5 %reduce-scatter.3.cloned.1.call-start = ((), (), s32[]{:S(2)}) async-start(), calls=%async_computation.2 | async-start | bytes 1310720 | tf_op jit(solution)/shard_map/reduce_scatter | solution.py:375
  31.0 3.8 copy-start
  31.1 160.1 %all-reduce.4.cloned.1.call-start = ((), (), s32[]{:S(2)}) async-start(), calls=%async_computation.3 | async-start | bytes 2097152 | tf_op jit(solution)/shard_map/psum | solution.py:396
  131.4 120.4 %all-reduce.6.cloned.1.call-start = ((), (), s32[]{:S(2)}) async-start(), calls=%async_computation.4 | async-start | bytes 2097152 | tf_op jit(solution)/shard_map/psum | solution.py:396
  148.5 42.7 %copy-start.3 = (bf16[1,512,512]{2,1,0:T(8,128)(2,1)S(1)}, bf16[1,512,512]{2,1,0:T(8,128)(2,1)}, u32[]{:S(2)}) copy-start(bf16[1,512,512]{2,1,0:T(8,128)(2,1)} %get-tuple-element.31) | copy-start | bytes 1572868
  148.5 42.7 %copy-start.4 = (bf16[1,512,512]{2,1,0:T(8,128)(2,1)S(1)}, bf16[1,512,512]{2,1,0:T(8,128)(2,1)}, u32[]{:S(2)}) copy-start(bf16[1,512,512]{2,1,0:T(8,128)(2,1)} %get-tuple-element.38) | copy-start | bytes 1572868
  191.1 127.2 %all-reduce.8.cloned.1.call-start = ((), (), s32[]{:S(2)}) async-start(), calls=%async_computation.5 | async-start | bytes 4194304 | tf_op jit(solution)/shard_map/psum | solution.py:396
  193.7 58.2 %copy-start.1 = (bf16[1,512,512]{2,1,0:T(8,128)(2,1)S(1)}, bf16[1,512,512]{2,1,0:T(8,128)(2,1)}, u32[]{:S(2)}) copy-start(bf16[1,512,512]{2,1,0:T(8,128)(2,1)} %get-tuple-element.32) | copy-start | bytes 1572868
  193.7 58.2 %copy-start.2 = (bf16[1,512,512]{2,1,0:T(8,128)(2,1)S(1)}, bf16[1,512,512]{2,1,0:T(8,128)(2,1)}, u32[]{:S(2)}) copy-start(bf16[1,512,512]{2,1,0:T(8,128)(2,1)} %get-tuple-element.33) | copy-start | bytes 1572868
  251.8 144.2 %reduce-scatter.5.cloned.1.call-start = ((), (), s32[]{:S(2)}) async-start(), calls=%async_computation.6 | async-start | bytes 1310720 | tf_op jit(solution)/shard_map/reduce_scatter | solution.py:375
Sparse Core Ops, SparseCore 0:
  31.2 29.9 reduce-scatter.2
  131.5 59.5 all-reduce.3
  193.5 58.2 all-reduce.5
  254.0 64.2 all-reduce.7
  368.5 27.5 reduce-scatter.4
